TPU v7x, 256 devices: a whole 4x4x8 slice. The times are simulated.
256 devices in a mesh: sp: 8 (over z), dp: 32 (over x, y, core).
Axes of the slice: x: 4, y: 4, z: 8, core: 2. Of those that a mesh axis runs over, the one named last changes fastest.
Arguments:
- hidden_states: bfloat16 [32, 2048, 8192], P('dp', 'sp'), may hold values from -6 to 6
- queries: bfloat16 [32, 2048, 4096], P('dp', 'sp'), may hold values from -360 to 360
- norm_gain: bfloat16 [8192], replicated, may hold values from 0.5 to 1.5
- key_value_matrix: bfloat16 [8192, 1024], P('dp'), may hold values from -0.0625 to 0.0625
- trace_offsets: int32 [32, 9], P('dp'), may hold values from 0 to 2048, as said below
- token_order: int32 [32, 2048], P('dp'), may hold values from 0 to 2047, each once within a row
Outputs:
- attended: bfloat16 [32, 2048, 4096], P('dp', 'sp')
Inputs may be any that keep to these rules, and one draw needn't show every extreme that they name: Each row rises strictly from 0 to 2048; trace t of pack p holds the positions from trace_offsets[p, t] to trace_offsets[p, t + 1] - 1. `token_order`: each row is a permutation of the 2048 positions of its pack.
All inputs are finite; a program needn't handle non-finite values.
Results may differ from a plain program's by a relative error of at most 0.0034.
The roundings to bfloat16 on the way count: a program that leaves them out, or rounds other values in their place, can miss the bound.
Values may be sent and summed in bfloat16 or wider, within the bound.
No kernel may reach another device: no remote copies, remote signals or barrier semaphores. Data moves between devices by JAX's collectives and lax.ppermute only.
A program may use at most 128 MiB of HBM per device.

v0:
```python
import math
import jax
import jax.numpy as jnp
from jax import lax
from jax.sharding import PartitionSpec as P

QUERY_HEADS = 32
KEY_VALUE_HEADS = 4
HEAD_SIZE = 128
EPSILON = 1e-05
ROPE_BASE = 500000.0


def locate(positions, starts):
    inside = starts[None, :] <= positions[:, None]
    trace_ids = jnp.sum(inside.astype(jnp.int32), axis=1) - 1
    begin = jnp.max(jnp.where(inside, starts[None, :], 0), axis=1)
    return (trace_ids, positions - begin)


def rotate(vectors, within):
    half = vectors.shape[-1] // 2
    index = jnp.arange(half, dtype=jnp.float32)
    freqs = jnp.exp(index * (-2.0 * math.log(ROPE_BASE) / vectors.shape[-1]))
    angles = within.astype(jnp.float32)[:, None] * freqs[None, :]
    cosine = jnp.cos(angles)[:, None, :]
    sine = jnp.sin(angles)[:, None, :]
    first = vectors[..., :half]
    second = vectors[..., half:]
    return jnp.concatenate(
        [first * cosine - second * sine, second * cosine + first * sine], axis=-1
    )


def normalize(rows, gain):
    value_rows = rows.astype(jnp.float32)
    scale = lax.rsqrt(jnp.mean(value_rows * value_rows, axis=-1, keepdims=True) + EPSILON)
    return (value_rows * scale * gain.astype(jnp.float32)).astype(jnp.bfloat16)


def on_device(hidden_states, queries, norm_gain, key_value_matrix, trace_offsets, token_order):
    sequence_parallel_count = lax.axis_size("sp")
    my_index = lax.axis_index("sp")
    resident_rows = hidden_states.shape[1]
    all_rows = resident_rows * sequence_parallel_count
    normed = normalize(hidden_states[0], norm_gain)
    projected_rows = jnp.dot(
        normed,
        lax.all_gather(key_value_matrix, "dp", axis=0, tiled=True),
        preferred_element_type=jnp.float32,
    )
    starts = trace_offsets[0]
    positions = token_order[0]
    trace_ids, within = locate(positions, starts)
    own_within = lax.dynamic_slice_in_dim(within, my_index * resident_rows, resident_rows, 0)
    head_slices = rotate(
        queries[0].astype(jnp.float32).reshape(resident_rows, QUERY_HEADS, HEAD_SIZE), own_within
    ).astype(jnp.bfloat16)
    key_value_pairs = projected_rows.reshape(resident_rows, KEY_VALUE_HEADS, 2, HEAD_SIZE)
    key_rows = rotate(key_value_pairs[:, :, 0], own_within).astype(jnp.bfloat16)
    value_rows = key_value_pairs[:, :, 1].astype(jnp.bfloat16)
    query_groups = max(KEY_VALUE_HEADS, sequence_parallel_count)
    stacked_rows = jnp.repeat(
        jnp.stack((key_rows, value_rows), axis=2), query_groups // KEY_VALUE_HEADS, axis=1
    ).reshape(resident_rows, query_groups * 2 * HEAD_SIZE)
    moved_queries, moved_pairs = (
        lax.all_to_all(
            head_slices.reshape(resident_rows, QUERY_HEADS * HEAD_SIZE),
            "sp",
            split_axis=1,
            concat_axis=0,
            tiled=True,
        ),
        lax.all_to_all(stacked_rows, "sp", split_axis=1, concat_axis=0, tiled=True),
    )
    local_groups = query_groups // sequence_parallel_count
    local_heads = QUERY_HEADS // sequence_parallel_count
    per_group = local_heads // local_groups
    moved_queries = moved_queries.reshape(all_rows, local_groups, per_group, HEAD_SIZE)
    moved_pairs = moved_pairs.reshape(all_rows, local_groups, 2, HEAD_SIZE)
    keys_all = moved_pairs[:, :, 0]
    values_all = moved_pairs[:, :, 1]
    width = min(512, all_rows)

    def block(block_index):
        first_row = block_index * width
        query_block = lax.dynamic_slice_in_dim(moved_queries, first_row, width, 0)
        block_ids = lax.dynamic_slice_in_dim(trace_ids, first_row, width, 0)
        block_positions = lax.dynamic_slice_in_dim(positions, first_row, width, 0)
        scores = jnp.einsum(
            "bgpd,kgd->gpbk", query_block, keys_all, preferred_element_type=jnp.float32
        ) / math.sqrt(HEAD_SIZE)
        mask = (block_ids[:, None] == trace_ids[None, :]) & (
            positions[None, :] <= block_positions[:, None]
        )
        scores = jnp.where(mask, scores, -1e30)
        peak = jnp.max(scores, axis=-1, keepdims=True)
        expo = jnp.where(mask, jnp.exp(scores - peak), 0.0)
        totals = jnp.sum(expo, axis=-1)
        weights = expo.astype(jnp.bfloat16)
        mixed = jnp.einsum(
            "gpbk,kgd->bgpd", weights, values_all, preferred_element_type=jnp.float32
        )
        result = mixed / jnp.transpose(totals, (2, 0, 1))[..., None]
        return result.astype(jnp.bfloat16).reshape(width, local_heads * HEAD_SIZE)

    attended = lax.map(block, jnp.arange(all_rows // width, dtype=jnp.int32)).reshape(
        all_rows, local_heads * HEAD_SIZE
    )
    returned = lax.all_to_all(attended, "sp", split_axis=0, concat_axis=1, tiled=True)
    return returned[None]


def solution(mesh):
    return jax.shard_map(
        on_device,
        mesh=mesh,
        in_specs=(
            P("dp", "sp", None),
            P("dp", "sp", None),
            P(),
            P("dp", None),
            P("dp", None),
            P("dp", None),
        ),
        out_specs=P("dp", "sp", None),
        check_vma=False,
    )
```

profile of v0, /device:TPU:1, one launch (start us, length us, event | category | flops | bytes accessed | tf_op | source)
XLA Modules:
  0.0 302.1 jit_solution(7556706558653838073)
XLA Ops:
  7.3 4.3 %copy.44 = f32[1,256,4096]{1,2,0:T(8,128)} copy(bf16[1,256,4096]{2,1,0:T(8,128)(2,1)} %param.9) | data formatting | bytes 6291456 | tf_op jit(solution)/shard_map/convert_element_type | solution.py:57
  16.6 9.0 %all-to-all-start = ((bf16[256,8,512]{0,2,1:T(8,128)(2,1)}), bf16[256,8,512]{0,2,1:T(8,128)(2,1)S(1)}, u32[]{:S(2)}, u32[]{:S(2)}) async-start(bf16[256,8,512]{0,2,1:T(8,128)(2,1)} %bitcast.126), calls=%async_computation | async-start | bytes 4194304 | tf_op jit(solution)/shard_map/all_to_all | solution.py:67
  25.6 3.4 %fusion.21 = f32[256]{0:T(256)S(1)} fusion(bf16[1,256,8192]{2,1,0:T(8,128)(2,1)} %param.8), kind=kLoop, calls=%fused_computation.23 | loop fusion | flops 6291200 | bytes 4195328 | tf_op jit(solution)/shard_map/reduce_sum | solution.py:37
  29.0 62.8 %all-gather.2.cloned.1.call-done = bf16[8192,1024]{1,0:T(8,128)(2,1)} async-done(((bf16[256,1024]{1,0:T(8,128)(2,1)}), bf16[8192,1024]{1,0:T(8,128)(2,1)}) %all-gather.2.cloned.1.call-update) | async-done | bytes 16777232 | tf_op jit(solution)/shard_map/all_gather | solution.py:49
  91.7 21.3 %copy.46 = bf16[1024,8192]{1,0:T(8,128)(2,1)} copy(bf16[1024,8192]{0,1:T(8,128)(2,1)} %bitcast.121) | data formatting | bytes 33554432 | tf_op jit(solution)/shard_map/dot_general | solution.py:47
  113.1 9.5 %fusion.25 = f32[256,4,2,128]{0,3,2,1:T(8,128)S(1)} fusion(bf16[4,2,128,8192]{3,2,1,0:T(8,128)(2,1)} %bitcast.122, bf16[1,256,8192]{2,1,0:T(8,128)(2,1)} %param.8, f32[8192]{0:T(1024)S(1)} %convert_element_type.56, f32[256]{0:T(256)S(1)} %add_rsqrt_fusion), kind=kOutput, calls=%fused_computation.27 | convolution fusion | flops 4303355904 | bytes 22053888 | tf_op jit(solution)/shard_map/dot_general | solution.py:47
  123.9 6.7 %all-to-all-start.1 = ((bf16[256,8,256]{0,2,1:T(8,128)(2,1)}), bf16[256,8,256]{0,2,1:T(8,128)(2,1)S(1)}, u32[]{:S(2)}, u32[]{:S(2)}) async-start(bf16[256,8,256]{0,2,1:T(8,128)(2,1)} %bitcast.130), calls=%async_computation.1 | async-start | bytes 2097152 | tf_op jit(solution)/shard_map/all_to_all | solution.py:74
  133.1 4.2 %reshape.170 = bf16[2048,1,4,128]{0,3,2,1:T(8,128)(2,1)} reshape(bf16[8,256,512]{1,0,2:T(8,128)(2,1)} %copy.45) | data formatting | bytes 4194304 | tf_op jit(solution)/shard_map/reshape | solution.py:79
  137.3 22.5 %all-to-all-done.1 = bf16[256,8,256]{0,2,1:T(8,128)(2,1)S(1)} async-done(((bf16[256,8,256]{0,2,1:T(8,128)(2,1)}), bf16[256,8,256]{0,2,1:T(8,128)(2,1)S(1)}, u32[]{:S(2)}, u32[]{:S(2)}) %all-to-all-start.1) | async-done | bytes 1048608 | tf_op jit(solution)/shard_map/all_to_all | solution.py:74
  161.4 72.4 %while.10 = (s32[]{:T(128)}, bf16[4,512,512]{2,1,0:T(8,128)(2,1)}, s32[4]{0:T(128)S(1)}, s32[2048]{0:T(1024)S(1)}, s32[1,2048]{1,0:T(1,128)S(1)}, /*index=5*/s32...) while((s32[]{:T(128)}, bf16[4,512,512]{2,1,0:T(8,128)(2,1)}, ...), condition=%wide.region_6.7_spmd, body=%wide.region_3.6_spmd.sunk | while | flops 2205675520 | bytes 58790092 | solution.py:107
  163.6 4.9 %fusion.41 = (f32[4,512]{1,0:T(4,128)S(1)}, f32[512,4,2048]{2,0,1:T(8,128)S(1)}) fusion(pred[512,2048]{1,0:T(8,128)(4,1)S(1)} %compare_and_fusion.2, bf16[2048,1,128]{2,0,1:T(8,128)(2,1)S(1)} %get-tuple-element.211, bf16[2048,1,4,128]{0,3,2,1:T(8,128)(2,1)} %get-tuple-element.210, s32[]{:T(128)S(6)} %select_n.63), kind=kOutput, calls=%fused_computation.2.clone.1 | convolution fusion | flops 1086322688 | bytes 18882564 | tf_op jit(solution)/shard_map/while/body/eval_jaxpr/bgpd,kgd->gpbk/dot_general | solution.py:90
  168.5 5.0 %fusion.42 = f32[4,512]{1,0:T(4,128)S(1)} fusion(f32[512,4,2048]{2,0,1:T(8,128)S(1)} %get-tuple-element.176, f32[4,512]{1,0:T(4,128)S(1)} %get-tuple-element.177, pred[512,2048]{1,0:T(8,128)(4,1)S(1)} %compare_and_fusion.2), kind=kLoop, calls=%fused_computation.3.clone.1 | loop fusion | flops 20969472 | bytes 17842176 | tf_op jit(solution)/shard_map/while/body/eval_jaxpr/reduce_sum | solution.py:99
  173.5 4.9 %divide_convert_fusion.2 = bf16[512,1,4,128]{0,3,2,1:T(8,128)(2,1)S(1)} fusion(f32[512,4,2048]{2,0,1:T(8,128)S(1)} %get-tuple-element.176, f32[4,512]{1,0:T(4,128)S(1)} %get-tuple-element.177, pred[512,2048]{1,0:T(8,128)(4,1)S(1)} %compare_and_fusion.2, bf16[2048,1,128]{0,2,1:T(8,128)(2,1)S(1)} %get-tuple-element.212, f32[512,4]{0,1:T(4,128)S(1)} %bitcast.137), kind=kOutput, calls=%fused_computation.10.clone.1 | convolution fusion | flops 1095237632 | bytes 18890752 | tf_op jit(solution)/shard_map/while/body/eval_jaxpr/gpbk,kgd->bgpd/dot_general | solution.py:101
  181.7 4.9 %fusion.41 = (f32[4,512]{1,0:T(4,128)S(1)}, f32[512,4,2048]{2,0,1:T(8,128)S(1)}) fusion(pred[512,2048]{1,0:T(8,128)(4,1)S(1)} %compare_and_fusion.2, bf16[2048,1,128]{2,0,1:T(8,128)(2,1)S(1)} %get-tuple-element.211, bf16[2048,1,4,128]{0,3,2,1:T(8,128)(2,1)} %get-tuple-element.210, s32[]{:T(128)S(6)} %select_n.63), kind=kOutput, calls=%fused_computation.2.clone.1 | convolution fusion | flops 1086322688 | bytes 18882564 | tf_op jit(solution)/shard_map/while/body/eval_jaxpr/bgpd,kgd->gpbk/dot_general | solution.py:90
  186.6 5.0 %fusion.42 = f32[4,512]{1,0:T(4,128)S(1)} fusion(f32[512,4,2048]{2,0,1:T(8,128)S(1)} %get-tuple-element.176, f32[4,512]{1,0:T(4,128)S(1)} %get-tuple-element.177, pred[512,2048]{1,0:T(8,128)(4,1)S(1)} %compare_and_fusion.2), kind=kLoop, calls=%fused_computation.3.clone.1 | loop fusion | flops 20969472 | bytes 17842176 | tf_op jit(solution)/shard_map/while/body/eval_jaxpr/reduce_sum | solution.py:99
  191.6 4.9 %divide_convert_fusion.2 = bf16[512,1,4,128]{0,3,2,1:T(8,128)(2,1)S(1)} fusion(f32[512,4,2048]{2,0,1:T(8,128)S(1)} %get-tuple-element.176, f32[4,512]{1,0:T(4,128)S(1)} %get-tuple-element.177, pred[512,2048]{1,0:T(8,128)(4,1)S(1)} %compare_and_fusion.2, bf16[2048,1,128]{0,2,1:T(8,128)(2,1)S(1)} %get-tuple-element.212, f32[512,4]{0,1:T(4,128)S(1)} %bitcast.137), kind=kOutput, calls=%fused_computation.10.clone.1 | convolution fusion | flops 1095237632 | bytes 18890752 | tf_op jit(solution)/shard_map/while/body/eval_jaxpr/gpbk,kgd->bgpd/dot_general | solution.py:101
  199.8 4.9 %fusion.41 = (f32[4,512]{1,0:T(4,128)S(1)}, f32[512,4,2048]{2,0,1:T(8,128)S(1)}) fusion(pred[512,2048]{1,0:T(8,128)(4,1)S(1)} %compare_and_fusion.2, bf16[2048,1,128]{2,0,1:T(8,128)(2,1)S(1)} %get-tuple-element.211, bf16[2048,1,4,128]{0,3,2,1:T(8,128)(2,1)} %get-tuple-element.210, s32[]{:T(128)S(6)} %select_n.63), kind=kOutput, calls=%fused_computation.2.clone.1 | convolution fusion | flops 1086322688 | bytes 18882564 | tf_op jit(solution)/shard_map/while/body/eval_jaxpr/bgpd,kgd->gpbk/dot_general | solution.py:90
  204.7 5.0 %fusion.42 = f32[4,512]{1,0:T(4,128)S(1)} fusion(f32[512,4,2048]{2,0,1:T(8,128)S(1)} %get-tuple-element.176, f32[4,512]{1,0:T(4,128)S(1)} %get-tuple-element.177, pred[512,2048]{1,0:T(8,128)(4,1)S(1)} %compare_and_fusion.2), kind=kLoop, calls=%fused_computation.3.clone.1 | loop fusion | flops 20969472 | bytes 17842176 | tf_op jit(solution)/shard_map/while/body/eval_jaxpr/reduce_sum | solution.py:99
  209.7 4.9 %divide_convert_fusion.2 = bf16[512,1,4,128]{0,3,2,1:T(8,128)(2,1)S(1)} fusion(f32[512,4,2048]{2,0,1:T(8,128)S(1)} %get-tuple-element.176, f32[4,512]{1,0:T(4,128)S(1)} %get-tuple-element.177, pred[512,2048]{1,0:T(8,128)(4,1)S(1)} %compare_and_fusion.2, bf16[2048,1,128]{0,2,1:T(8,128)(2,1)S(1)} %get-tuple-element.212, f32[512,4]{0,1:T(4,128)S(1)} %bitcast.137), kind=kOutput, calls=%fused_computation.10.clone.1 | convolution fusion | flops 1095237632 | bytes 18890752 | tf_op jit(solution)/shard_map/while/body/eval_jaxpr/gpbk,kgd->bgpd/dot_general | solution.py:101
  217.9 4.9 %fusion.41 = (f32[4,512]{1,0:T(4,128)S(1)}, f32[512,4,2048]{2,0,1:T(8,128)S(1)}) fusion(pred[512,2048]{1,0:T(8,128)(4,1)S(1)} %compare_and_fusion.2, bf16[2048,1,128]{2,0,1:T(8,128)(2,1)S(1)} %get-tuple-element.211, bf16[2048,1,4,128]{0,3,2,1:T(8,128)(2,1)} %get-tuple-element.210, s32[]{:T(128)S(6)} %select_n.63), kind=kOutput, calls=%fused_computation.2.clone.1 | convolution fusion | flops 1086322688 | bytes 18882564 | tf_op jit(solution)/shard_map/while/body/eval_jaxpr/bgpd,kgd->gpbk/dot_general | solution.py:90
  222.8 5.0 %fusion.42 = f32[4,512]{1,0:T(4,128)S(1)} fusion(f32[512,4,2048]{2,0,1:T(8,128)S(1)} %get-tuple-element.176, f32[4,512]{1,0:T(4,128)S(1)} %get-tuple-element.177, pred[512,2048]{1,0:T(8,128)(4,1)S(1)} %compare_and_fusion.2), kind=kLoop, calls=%fused_computation.3.clone.1 | loop fusion | flops 20969472 | bytes 17842176 | tf_op jit(solution)/shard_map/while/body/eval_jaxpr/reduce_sum | solution.py:99
  227.8 4.9 %divide_convert_fusion.2 = bf16[512,1,4,128]{0,3,2,1:T(8,128)(2,1)S(1)} fusion(f32[512,4,2048]{2,0,1:T(8,128)S(1)} %get-tuple-element.176, f32[4,512]{1,0:T(4,128)S(1)} %get-tuple-element.177, pred[512,2048]{1,0:T(8,128)(4,1)S(1)} %compare_and_fusion.2, bf16[2048,1,128]{0,2,1:T(8,128)(2,1)S(1)} %get-tuple-element.212, f32[512,4]{0,1:T(4,128)S(1)} %bitcast.137), kind=kOutput, calls=%fused_computation.10.clone.1 | convolution fusion | flops 1095237632 | bytes 18890752 | tf_op jit(solution)/shard_map/while/body/eval_jaxpr/gpbk,kgd->bgpd/dot_general | solution.py:101
  233.8 55.0 %all_to_all.45 = bf16[8,256,512]{2,1,0:T(8,128)(2,1)S(1)} all-to-all(bf16[8,256,512]{2,1,0:T(8,128)(2,1)} %bitcast.131), channel_id=1, replica_groups=mesh['sp'=8,'dp'=32] {'sp'}, dimensions={0} | all-to-all | bytes 4194304 | tf_op jit(solution)/shard_map/all_to_all | solution.py:110
  291.2 4.1 %copy.54 = bf16[1,256,4096]{2,1,0:T(8,128)(2,1)} copy(bf16[1,256,4096]{1,2,0:T(8,128)(2,1)} %bitcast.128) | data formatting | bytes 4194304 | tf_op jit(solution)/shard_map/broadcast_in_dim | solution.py:111
  (55 shorter events, 24.0 us)
Async XLA Ops:
  6.5 5.1 %copy-start = (s32[1,2048]{1,0:T(1,128)S(1)}, s32[1,2048]{1,0:T(1,128)}, u32[]{:S(2)}) copy-start(s32[1,2048]{1,0:T(1,128)} %param.13) | copy-start | bytes 24580
  6.5 5.1 %copy-start.2 = (s32[1,9]{1,0:T(1,128)S(1)}, s32[1,9]{1,0:T(1,128)}, u32[]{:S(2)}) copy-start(s32[1,9]{1,0:T(1,128)} %param.12) | copy-start | bytes 112
  6.5 85.2 %all-gather.2.cloned.1.call-start = ((), (), s32[]{:S(2)}) async-start(), calls=%async_computation.3 | async-start | bytes 17301504 | tf_op jit(solution)/shard_map/all_gather | solution.py:49
  15.1 10.6 %copy-start.1 = (bf16[8192]{0:T(1024)(128)(2,1)S(1)}, bf16[8192]{0:T(1024)(128)(2,1)}, u32[]{:S(2)}) copy-start(bf16[8192]{0:T(1024)(128)(2,1)} %param.10) | copy-start | bytes 49156
  16.6 106.2 %all-to-all-start = ((bf16[256,8,512]{0,2,1:T(8,128)(2,1)}), bf16[256,8,512]{0,2,1:T(8,128)(2,1)S(1)}, u32[]{:S(2)}, u32[]{:S(2)}) async-start(bf16[256,8,512]{0,2,1:T(8,128)(2,1)} %bitcast.126), calls=%async_computation | async-start | bytes 4194304 | tf_op jit(solution)/shard_map/all_to_all | solution.py:67
  123.9 36.0 %all-to-all-start.1 = ((bf16[256,8,256]{0,2,1:T(8,128)(2,1)}), bf16[256,8,256]{0,2,1:T(8,128)(2,1)S(1)}, u32[]{:S(2)}, u32[]{:S(2)}) async-start(bf16[256,8,256]{0,2,1:T(8,128)(2,1)} %bitcast.130), calls=%async_computation.1 | async-start | bytes 2097152 | tf_op jit(solution)/shard_map/all_to_all | solution.py:74
Sparse Core Ops, SparseCore 0:
  9.9 81.8 all-gather.1
where the time goes:
time: 303 us; the launch traced here: 302 us
  waiting for transfers between devices  86 us (28%)
  blocking collectives  55 us (18%)
  matrix products  48.8 us (16%)
  local copies, waits for them, and re-layouts  48.4 us (16%)
  other arithmetic  32.3 us (11%)
  starting transfers between devices  15.7 us (5%)
  between operations  13.5 us (4%)
    all_gather x1, waiting for transfers between devices, on_device(): lax.all_gather(key_value_matrix, 'dp', axis=0, tiled=True)  62.8 us
    all_to_all x1, blocking collectives, on_device(): lax.all_to_all(attended, 'sp', split_axis=0, concat_axis=1, tiled=True)  55 us
    all_to_all x1, waiting for transfers between devices, on_device(): lax.all_to_all(stacked_rows, 'sp', split_axis=1, concat_axis=0, tiled=True)  22.5 us
    dot_general x1, local copies, waits for them, and re-layouts, on_device(): jnp.dot(normed, lax.all_gather(key_value_matrix, 'dp', axis=0, tiled=True...  21.3 us
    reduce_sum x4, other arithmetic, block(): totals = jnp.sum(expo, axis=-1)  20.1 us
    dot_general x4, matrix products, block(): jnp.einsum('gpbk,kgd->bgpd', weights, values_all, preferred_element_type=...  19.8 us
    dot_general x4, matrix products, block(): jnp.einsum('bgpd,kgd->gpbk', query_block, keys_all, preferred_element_typ...  19.5 us
    dot_general x1, matrix products, on_device(): jnp.dot(normed, lax.all_gather(key_value_matrix, 'dp', axis=0, tiled=True...  9.49 us
  transfers between devices with their start and end apart: 3, of which 2 were waited for; matrix products, arithmetic and copies ran while one was open for 17% of the time, Pallas kernels for 0%

commit v1 on v0

--- a/solution.py
+++ b/solution.py
@@ -46,7 +46,9 @@
     normed = normalize(hidden_states[0], norm_gain)
     projected_rows = jnp.dot(
         normed,
-        lax.all_gather(key_value_matrix, "dp", axis=0, tiled=True),
+        jnp.concatenate(
+            lax.all_to_all(jnp.stack([key_value_matrix] * lax.axis_size("dp")), "dp", 0, 0), axis=0
+        ),
         preferred_element_type=jnp.float32,
     )
     starts = trace_offsets[0]

time: 303 us -> 523 us (1.73)
  the two profiles are of different devices: /device:TPU:1 before, /device:TPU:13 now
where the time goes in v1:
time: 523 us; the launch traced here: 521 us
  waiting for transfers between devices  283 us (54%)
  local copies, waits for them, and re-layouts  76.9 us (15%)
  blocking collectives  55 us (11%)
  matrix products  48.8 us (9%)
  other arithmetic  32 us (6%)
  starting transfers between devices  22.8 us (4%)
    all_to_all x1, waiting for transfers between devices, on_device(): lax.all_to_all(jnp.stack([key_value_matrix] * lax.axis_size('dp')), 'dp',...  260 us
    all_to_all x1, blocking collectives, on_device(): lax.all_to_all(attended, 'sp', split_axis=0, concat_axis=1, tiled=True)  55 us
    all_to_all x1, local copies, waits for them, and re-layouts, on_device(): lax.all_to_all(jnp.stack([key_value_matrix] * lax.axis_size('dp')), 'dp',...  22.5 us
    all_to_all x1, waiting for transfers between devices, on_device(): lax.all_to_all(stacked_rows, 'sp', split_axis=1, concat_axis=0, tiled=True)  22.5 us
    dot_general x1, local copies, waits for them, and re-layouts, on_device(): jnp.dot(normed, jnp.concatenate(lax.all_to_all(jnp.stack([key_value_matri...  21.4 us
    reduce_sum x4, other arithmetic, block(): totals = jnp.sum(expo, axis=-1)  20.1 us
    dot_general x4, matrix products, block(): jnp.einsum('gpbk,kgd->bgpd', weights, values_all, preferred_element_type=...  19.8 us
    dot_general x4, matrix products, block(): jnp.einsum('bgpd,kgd->gpbk', query_block, keys_all, preferred_element_typ...  19.5 us
  transfers between devices with their start and end apart: 3, of which 2 were waited for; matrix products, arithmetic and copies ran while one was open for 14% of the time, Pallas kernels for 0%

profile of v1, /device:TPU:13, one launch (start us, length us, event | category | flops | bytes accessed | tf_op | source)
XLA Modules:
  0.0 521.0 jit_solution(14578546628405399335)
XLA Ops:
  1.2 6.0 %stack.4 = bf16[32,256,1024]{1,2,0:T(8,128)(2,1)} broadcast(bf16[256,1024]{0,1:T(8,128)(2,1)S(1)} %copy.59), dimensions={1,2} | broadcast | bytes 17301504 | tf_op jit(solution)/shard_map/stack | solution.py:50
  7.2 8.0 %all-to-all-start.1 = ((bf16[32,256,1024]{1,2,0:T(8,128)(2,1)}), bf16[32,256,1024]{1,2,0:T(8,128)(2,1)}, u32[]{:S(2)}, u32[]{:S(2)}) async-start(bf16[32,256,1024]{1,2,0:T(8,128)(2,1)} %stack.4), calls=%async_computation.1 | async-start | bytes 33554432 | tf_op jit(solution)/shard_map/all_to_all | solution.py:50
  23.2 260.4 %all-to-all-done.1 = bf16[32,256,1024]{1,2,0:T(8,128)(2,1)} async-done(((bf16[32,256,1024]{1,2,0:T(8,128)(2,1)}), bf16[32,256,1024]{1,2,0:T(8,128)(2,1)}, u32[]{:S(2)}, u32[]{:S(2)}) %all-to-all-start.1) | async-done | bytes 16777248 | tf_op jit(solution)/shard_map/all_to_all | solution.py:50
  283.6 8.2 %all-to-all-start = ((bf16[256,8,512]{0,2,1:T(8,128)(2,1)}), bf16[256,8,512]{0,2,1:T(8,128)(2,1)S(1)}, u32[]{:S(2)}, u32[]{:S(2)}) async-start(bf16[256,8,512]{0,2,1:T(8,128)(2,1)} %bitcast.128), calls=%async_computation | async-start | bytes 4194304 | tf_op jit(solution)/shard_map/all_to_all | solution.py:69
  294.9 22.5 %copy.60 = bf16[32,256,1024]{2,1,0:T(8,128)(2,1)} copy(bf16[32,256,1024]{1,2,0:T(8,128)(2,1)} %all-to-all-done.1) | data formatting | bytes 33554432 | tf_op jit(solution)/shard_map/all_to_all | solution.py:50
  317.5 21.4 %copy.61 = bf16[1024,8192]{1,0:T(8,128)(2,1)} copy(bf16[1024,8192]{0,1:T(8,128)(2,1)} %bitcast.123) | data formatting | bytes 33554432 | tf_op jit(solution)/shard_map/dot_general | solution.py:47
  338.9 9.5 %fusion.25 = f32[256,4,2,128]{0,3,2,1:T(8,128)S(1)} fusion(bf16[4,2,128,8192]{3,2,1,0:T(8,128)(2,1)} %bitcast.124, bf16[1,256,8192]{2,1,0:T(8,128)(2,1)} %param.8, f32[8192]{0:T(1024)S(1)} %convert_element_type.56, f32[256]{0:T(256)S(1)} %add_rsqrt_fusion), kind=kOutput, calls=%fused_computation.27 | convolution fusion | flops 4303355904 | bytes 22053888 | tf_op jit(solution)/shard_map/dot_general | solution.py:47
  349.7 6.6 %all-to-all-start.2 = ((bf16[256,8,256]{0,2,1:T(8,128)(2,1)}), bf16[256,8,256]{0,2,1:T(8,128)(2,1)S(1)}, u32[]{:S(2)}, u32[]{:S(2)}) async-start(bf16[256,8,256]{0,2,1:T(8,128)(2,1)} %bitcast.132), calls=%async_computation.2 | async-start | bytes 2097152 | tf_op jit(solution)/shard_map/all_to_all | solution.py:76
  358.8 4.2 reshape.175
  363.0 22.5 %all-to-all-done.2 = bf16[256,8,256]{0,2,1:T(8,128)(2,1)S(1)} async-done(((bf16[256,8,256]{0,2,1:T(8,128)(2,1)}), bf16[256,8,256]{0,2,1:T(8,128)(2,1)S(1)}, u32[]{:S(2)}, u32[]{:S(2)}) %all-to-all-start.2) | async-done | bytes 1048608 | tf_op jit(solution)/shard_map/all_to_all | solution.py:76
  387.0 72.4 %while.10 = (s32[]{:T(128)}, bf16[4,512,512]{2,1,0:T(8,128)(2,1)}, s32[4]{0:T(128)S(1)}, s32[2048]{0:T(1024)S(1)}, s32[1,2048]{1,0:T(1,128)S(1)}, /*index=5*/s32...) while((s32[]{:T(128)}, bf16[4,512,512]{2,1,0:T(8,128)(2,1)}, ...), condition=%wide.region_6.7_spmd, body=%wide.region_3.6_spmd.sunk | while | flops 2205675520 | bytes 58790592 | solution.py:109
  389.2 4.9 fusion.41
  394.1 5.0 fusion.42
  399.2 4.9 divide_convert_fusion.2
  407.4 4.9 fusion.41
  412.2 5.0 fusion.42
  417.3 4.9 divide_convert_fusion.2
  425.5 4.9 fusion.41
  430.3 5.0 fusion.42
  435.4 4.9 divide_convert_fusion.2
  443.6 4.9 fusion.41
  448.4 5.0 fusion.42
  453.5 4.9 divide_convert_fusion.2
  459.5 55.0 %all_to_all.50 = bf16[8,256,512]{2,1,0:T(8,128)(2,1)S(1)} all-to-all(bf16[8,256,512]{2,1,0:T(8,128)(2,1)} %bitcast.133), channel_id=1, replica_groups=mesh['sp'=8,'dp'=32] {'sp'}, dimensions={0} | all-to-all | bytes 4194304 | tf_op jit(solution)/shard_map/all_to_all | solution.py:112
  (59 shorter events, 34.7 us)
Async XLA Ops:
  7.2 8.0 %copy-start = (bf16[1,256,4096]{2,1,0:T(8,128)(2,1)S(1)}, bf16[1,256,4096]{2,1,0:T(8,128)(2,1)}, u32[]{:S(2)}) copy-start(bf16[1,256,4096]{2,1,0:T(8,128)(2,1)} %param.9) | copy-start | bytes 6291460
  7.2 276.4 %all-to-all-start.1 = ((bf16[32,256,1024]{1,2,0:T(8,128)(2,1)}), bf16[32,256,1024]{1,2,0:T(8,128)(2,1)}, u32[]{:S(2)}, u32[]{:S(2)}) async-start(bf16[32,256,1024]{1,2,0:T(8,128)(2,1)} %stack.4), calls=%async_computation.1 | async-start | bytes 33554432 | tf_op jit(solution)/shard_map/all_to_all | solution.py:50
  15.2 3.0 copy-start.1
  15.2 3.0 copy-start.3
  21.7 270.1 %copy-start.2 = (bf16[8192]{0:T(1024)(128)(2,1)S(1)}, bf16[8192]{0:T(1024)(128)(2,1)}, u32[]{:S(2)}) copy-start(bf16[8192]{0:T(1024)(128)(2,1)} %param.10) | copy-start | bytes 49156
  283.6 65.0 %all-to-all-start = ((bf16[256,8,512]{0,2,1:T(8,128)(2,1)}), bf16[256,8,512]{0,2,1:T(8,128)(2,1)S(1)}, u32[]{:S(2)}, u32[]{:S(2)}) async-start(bf16[256,8,512]{0,2,1:T(8,128)(2,1)} %bitcast.128), calls=%async_computation | async-start | bytes 4194304 | tf_op jit(solution)/shard_map/all_to_all | solution.py:69
  349.7 35.8 %all-to-all-start.2 = ((bf16[256,8,256]{0,2,1:T(8,128)(2,1)}), bf16[256,8,256]{0,2,1:T(8,128)(2,1)S(1)}, u32[]{:S(2)}, u32[]{:S(2)}) async-start(bf16[256,8,256]{0,2,1:T(8,128)(2,1)} %bitcast.132), calls=%async_computation.2 | async-start | bytes 2097152 | tf_op jit(solution)/shard_map/all_to_all | solution.py:76
